TPU v7x, 256 devices: a whole 4x4x8 slice. The times are simulated.
256 devices in a mesh: row: 16 (over z, core), col: 16 (over x, y).
Axes of the slice: x: 4, y: 4, z: 8, core: 2. Of those that a mesh axis runs over, the one named last changes fastest.
Arguments:
- rhs: float32 [16, 64, 128], P('col'), may hold values from -6 to 6
- diag_inv: float32 [16, 128, 128], P('col'), as said below
- panel: bfloat16 [16, 16, 128, 128], P('row', 'col'), may hold values from -0.09375 to 0.09375
- offdiag: bfloat16 [1024, 16, 128, 128], P('row', 'col'), may hold values from -0.015625 to 0.015625
- known: bfloat16 [512, 64, 128], P(('row', 'col')), may hold values from -6 to 6
- row_index: int32 [1024], P('row'), may hold values from 0 to 31
Outputs:
- solution: bfloat16 [16, 64, 128], P('col')
Inputs may be any that keep to these rules, and one draw needn't show every extreme that they name: Each block of diag_inv is lower triangular (the inverse of a lower triangular diagonal block).
All inputs are finite; a program needn't handle non-finite values.
Results may differ from a plain program's by a relative error of at most 0.015.
Values may be sent and summed in bfloat16 or wider, within the bound.
A program may use at most 64 MiB of HBM per device.

v0:
```python
import jax
import jax.numpy as jnp
from jax import lax
from jax.sharding import PartitionSpec as P

NB = 16


def spread(array, axis, root):
    mine = lax.axis_index(axis) == root
    return lax.psum(jnp.where(mine, array, jnp.zeros_like(array)), axis)


def finish_block(total, inverse, turn_block, root, solved):
    local = jnp.dot(
        total, inverse, precision=lax.Precision.HIGHEST, preferred_element_type=jnp.float32
    ).astype(jnp.bfloat16)
    block = spread(local, "col", root)
    solved = lax.dynamic_update_index_in_dim(solved, block, turn_block, 0)
    return (block, solved)


def body(rhs, diag_inv, panel, offdiag, known, row_index):
    rows_count = lax.axis_size("row")
    cols_count = lax.axis_size("col")
    row_id = lax.axis_index("row")
    col_id = lax.axis_index("col")
    col_slots = NB // cols_count
    known_row = lax.all_gather(known, "col", axis=0, tiled=True)
    picked = jnp.take(known_row, row_index, axis=0)
    off_part = jnp.einsum("pqi,pbia->bqa", picked, offdiag, preferred_element_type=jnp.float32)
    off_sum = lax.psum(off_part, "row")
    update = rhs - off_sum
    col_global = jnp.arange(col_slots) * cols_count + col_id
    accum = jnp.zeros(update.shape, jnp.float32)
    solved = jnp.zeros((NB,) + update.shape[1:], jnp.bfloat16)

    def step_reduced(turn, carry):
        sums, result = carry
        block_id = NB - 1 - turn
        slot = block_id // cols_count
        partial_value = lax.dynamic_index_in_dim(sums, slot, 0, keepdims=False)
        summed = lax.psum(partial_value.astype(jnp.bfloat16), "row").astype(jnp.float32)
        total = lax.dynamic_index_in_dim(update, slot, 0, keepdims=False) - summed
        inverse = lax.dynamic_index_in_dim(diag_inv, slot, 0, keepdims=False)
        block, result = finish_block(total, inverse, block_id, block_id % cols_count, result)
        tiles = lax.dynamic_index_in_dim(panel, block_id // rows_count, 0, keepdims=False)
        contrib = jnp.einsum("qi,bia->bqa", block, tiles, preferred_element_type=jnp.float32)
        keep = (col_global < block_id) & (block_id % rows_count == row_id)
        return (sums + jnp.where(keep[:, None, None], contrib, 0.0), result)

    accum, solved = lax.fori_loop(0, NB, step_reduced, (accum, solved))
    return jnp.take(solved, col_global, axis=0)


def solution(mesh):
    placed = (
        P("col", None, None),
        P("col", None, None),
        P("row", "col", None, None),
        P("row", "col", None, None),
        P(("row", "col"), None, None),
        P("row"),
    )
    return jax.shard_map(
        body, mesh=mesh, in_specs=placed, out_specs=P("col", None, None), check_vma=False
    )
```

profile of v0, /device:TPU:0, one launch (start us, length us, event | category | flops | bytes accessed | tf_op | source)
XLA Modules:
  0.0 1928.7 jit_solution(12652828160161664547)
XLA Ops:
  26.9 48.6 %psum.35 = f32[1,64,128]{2,1,0:T(8,128)S(1)} all-reduce(f32[1,64,128]{2,1,0:T(8,128)S(1)} %fusion.9), channel_id=1, replica_groups=mesh['row'=16,'col'=16] {'row'}, use_global_device_ids=true, to_apply=%region_0.1 | all-reduce | flops 8192 | bytes 65536 | tf_op jit(solution)/shard_map/psum | solution.py:32
  75.6 1852.5 %while.19 = (s32[]{:T(128)}, f32[1,64,128]{2,1,0:T(8,128)S(1)}, bf16[16,64,128]{2,1,0:T(8,128)(2,1)S(1)}, s32[1]{0:T(128)}, s32[]{:T(128)}, /*index=5*/f32[1,64,...) while((s32[]{:T(128)}, f32[1,64,128]{2,1,0:T(8,128)S(1)}, ...), condition=%wide.region_4.5_spmd.clone, body=%wide.region_1.0_spmd.clone.sunk | while | flops 14762007 | bytes 393562 | solution.py:52
  75.6 45.7 %psum.40 = bf16[64,128]{1,0:T(8,128)(2,1)S(1)} all-reduce(bf16[64,128]{1,0:T(8,128)(2,1)S(1)} %fusion.26), channel_id=1, replica_groups=mesh['row'=16,'col'=16] {'row'}, use_global_device_ids=true, to_apply=%region_2.2 | all-reduce | flops 8192 | bytes 32768 | tf_op jit(solution)/shard_map/while/body/eval_jaxpr/psum | solution.py:43
  121.5 72.1 %psum.41 = bf16[64,128]{1,0:T(8,128)(2,1)S(1)} all-reduce(bf16[64,128]{1,0:T(8,128)(2,1)S(1)} %fusion.27), channel_id=1, replica_groups=mesh['row'=16,'col'=16] {'col'}, use_global_device_ids=true, to_apply=%region_3.3 | all-reduce | flops 8192 | bytes 32768 | tf_op jit(solution)/shard_map/while/body/eval_jaxpr/psum | solution.py:11
  239.7 69.6 %psum.41 = bf16[64,128]{1,0:T(8,128)(2,1)S(1)} all-reduce(bf16[64,128]{1,0:T(8,128)(2,1)S(1)} %fusion.27), channel_id=1, replica_groups=mesh['row'=16,'col'=16] {'col'}, use_global_device_ids=true, to_apply=%region_3.3 | all-reduce | flops 8192 | bytes 32768 | tf_op jit(solution)/shard_map/while/body/eval_jaxpr/psum | solution.py:11
  309.4 45.7 %psum.40 = bf16[64,128]{1,0:T(8,128)(2,1)S(1)} all-reduce(bf16[64,128]{1,0:T(8,128)(2,1)S(1)} %fusion.26), channel_id=1, replica_groups=mesh['row'=16,'col'=16] {'row'}, use_global_device_ids=true, to_apply=%region_2.2 | all-reduce | flops 8192 | bytes 32768 | tf_op jit(solution)/shard_map/while/body/eval_jaxpr/psum | solution.py:43
  355.3 69.6 %psum.41 = bf16[64,128]{1,0:T(8,128)(2,1)S(1)} all-reduce(bf16[64,128]{1,0:T(8,128)(2,1)S(1)} %fusion.27), channel_id=1, replica_groups=mesh['row'=16,'col'=16] {'col'}, use_global_device_ids=true, to_apply=%region_3.3 | all-reduce | flops 8192 | bytes 32768 | tf_op jit(solution)/shard_map/while/body/eval_jaxpr/psum | solution.py:11
  425.0 45.7 %psum.40 = bf16[64,128]{1,0:T(8,128)(2,1)S(1)} all-reduce(bf16[64,128]{1,0:T(8,128)(2,1)S(1)} %fusion.26), channel_id=1, replica_groups=mesh['row'=16,'col'=16] {'row'}, use_global_device_ids=true, to_apply=%region_2.2 | all-reduce | flops 8192 | bytes 32768 | tf_op jit(solution)/shard_map/while/body/eval_jaxpr/psum | solution.py:43
  470.9 69.6 %psum.41 = bf16[64,128]{1,0:T(8,128)(2,1)S(1)} all-reduce(bf16[64,128]{1,0:T(8,128)(2,1)S(1)} %fusion.27), channel_id=1, replica_groups=mesh['row'=16,'col'=16] {'col'}, use_global_device_ids=true, to_apply=%region_3.3 | all-reduce | flops 8192 | bytes 32768 | tf_op jit(solution)/shard_map/while/body/eval_jaxpr/psum | solution.py:11
  586.6 69.6 %psum.41 = bf16[64,128]{1,0:T(8,128)(2,1)S(1)} all-reduce(bf16[64,128]{1,0:T(8,128)(2,1)S(1)} %fusion.27), channel_id=1, replica_groups=mesh['row'=16,'col'=16] {'col'}, use_global_device_ids=true, to_apply=%region_3.3 | all-reduce | flops 8192 | bytes 32768 | tf_op jit(solution)/shard_map/while/body/eval_jaxpr/psum | solution.py:11
  702.2 69.6 %psum.41 = bf16[64,128]{1,0:T(8,128)(2,1)S(1)} all-reduce(bf16[64,128]{1,0:T(8,128)(2,1)S(1)} %fusion.27), channel_id=1, replica_groups=mesh['row'=16,'col'=16] {'col'}, use_global_device_ids=true, to_apply=%region_3.3 | all-reduce | flops 8192 | bytes 32768 | tf_op jit(solution)/shard_map/while/body/eval_jaxpr/psum | solution.py:11
  771.9 45.7 %psum.40 = bf16[64,128]{1,0:T(8,128)(2,1)S(1)} all-reduce(bf16[64,128]{1,0:T(8,128)(2,1)S(1)} %fusion.26), channel_id=1, replica_groups=mesh['row'=16,'col'=16] {'row'}, use_global_device_ids=true, to_apply=%region_2.2 | all-reduce | flops 8192 | bytes 32768 | tf_op jit(solution)/shard_map/while/body/eval_jaxpr/psum | solution.py:43
  817.8 69.6 %psum.41 = bf16[64,128]{1,0:T(8,128)(2,1)S(1)} all-reduce(bf16[64,128]{1,0:T(8,128)(2,1)S(1)} %fusion.27), channel_id=1, replica_groups=mesh['row'=16,'col'=16] {'col'}, use_global_device_ids=true, to_apply=%region_3.3 | all-reduce | flops 8192 | bytes 32768 | tf_op jit(solution)/shard_map/while/body/eval_jaxpr/psum | solution.py:11
  887.5 45.7 %psum.40 = bf16[64,128]{1,0:T(8,128)(2,1)S(1)} all-reduce(bf16[64,128]{1,0:T(8,128)(2,1)S(1)} %fusion.26), channel_id=1, replica_groups=mesh['row'=16,'col'=16] {'row'}, use_global_device_ids=true, to_apply=%region_2.2 | all-reduce | flops 8192 | bytes 32768 | tf_op jit(solution)/shard_map/while/body/eval_jaxpr/psum | solution.py:43
  933.4 69.6 %psum.41 = bf16[64,128]{1,0:T(8,128)(2,1)S(1)} all-reduce(bf16[64,128]{1,0:T(8,128)(2,1)S(1)} %fusion.27), channel_id=1, replica_groups=mesh['row'=16,'col'=16] {'col'}, use_global_device_ids=true, to_apply=%region_3.3 | all-reduce | flops 8192 | bytes 32768 | tf_op jit(solution)/shard_map/while/body/eval_jaxpr/psum | solution.py:11
  1049.0 69.6 %psum.41 = bf16[64,128]{1,0:T(8,128)(2,1)S(1)} all-reduce(bf16[64,128]{1,0:T(8,128)(2,1)S(1)} %fusion.27), channel_id=1, replica_groups=mesh['row'=16,'col'=16] {'col'}, use_global_device_ids=true, to_apply=%region_3.3 | all-reduce | flops 8192 | bytes 32768 | tf_op jit(solution)/shard_map/while/body/eval_jaxpr/psum | solution.py:11
  1118.7 45.7 %psum.40 = bf16[64,128]{1,0:T(8,128)(2,1)S(1)} all-reduce(bf16[64,128]{1,0:T(8,128)(2,1)S(1)} %fusion.26), channel_id=1, replica_groups=mesh['row'=16,'col'=16] {'row'}, use_global_device_ids=true, to_apply=%region_2.2 | all-reduce | flops 8192 | bytes 32768 | tf_op jit(solution)/shard_map/while/body/eval_jaxpr/psum | solution.py:43
  1164.7 69.6 %psum.41 = bf16[64,128]{1,0:T(8,128)(2,1)S(1)} all-reduce(bf16[64,128]{1,0:T(8,128)(2,1)S(1)} %fusion.27), channel_id=1, replica_groups=mesh['row'=16,'col'=16] {'col'}, use_global_device_ids=true, to_apply=%region_3.3 | all-reduce | flops 8192 | bytes 32768 | tf_op jit(solution)/shard_map/while/body/eval_jaxpr/psum | solution.py:11
  1280.3 69.6 %psum.41 = bf16[64,128]{1,0:T(8,128)(2,1)S(1)} all-reduce(bf16[64,128]{1,0:T(8,128)(2,1)S(1)} %fusion.27), channel_id=1, replica_groups=mesh['row'=16,'col'=16] {'col'}, use_global_device_ids=true, to_apply=%region_3.3 | all-reduce | flops 8192 | bytes 32768 | tf_op jit(solution)/shard_map/while/body/eval_jaxpr/psum | solution.py:11
  1395.9 69.6 %psum.41 = bf16[64,128]{1,0:T(8,128)(2,1)S(1)} all-reduce(bf16[64,128]{1,0:T(8,128)(2,1)S(1)} %fusion.27), channel_id=1, replica_groups=mesh['row'=16,'col'=16] {'col'}, use_global_device_ids=true, to_apply=%region_3.3 | all-reduce | flops 8192 | bytes 32768 | tf_op jit(solution)/shard_map/while/body/eval_jaxpr/psum | solution.py:11
  1511.5 69.6 %psum.41 = bf16[64,128]{1,0:T(8,128)(2,1)S(1)} all-reduce(bf16[64,128]{1,0:T(8,128)(2,1)S(1)} %fusion.27), channel_id=1, replica_groups=mesh['row'=16,'col'=16] {'col'}, use_global_device_ids=true, to_apply=%region_3.3 | all-reduce | flops 8192 | bytes 32768 | tf_op jit(solution)/shard_map/while/body/eval_jaxpr/psum | solution.py:11
  1627.1 69.6 %psum.41 = bf16[64,128]{1,0:T(8,128)(2,1)S(1)} all-reduce(bf16[64,128]{1,0:T(8,128)(2,1)S(1)} %fusion.27), channel_id=1, replica_groups=mesh['row'=16,'col'=16] {'col'}, use_global_device_ids=true, to_apply=%region_3.3 | all-reduce | flops 8192 | bytes 32768 | tf_op jit(solution)/shard_map/while/body/eval_jaxpr/psum | solution.py:11
  1742.7 69.6 %psum.41 = bf16[64,128]{1,0:T(8,128)(2,1)S(1)} all-reduce(bf16[64,128]{1,0:T(8,128)(2,1)S(1)} %fusion.27), channel_id=1, replica_groups=mesh['row'=16,'col'=16] {'col'}, use_global_device_ids=true, to_apply=%region_3.3 | all-reduce | flops 8192 | bytes 32768 | tf_op jit(solution)/shard_map/while/body/eval_jaxpr/psum | solution.py:11
  1858.4 69.6 %psum.41 = bf16[64,128]{1,0:T(8,128)(2,1)S(1)} all-reduce(bf16[64,128]{1,0:T(8,128)(2,1)S(1)} %fusion.27), channel_id=1, replica_groups=mesh['row'=16,'col'=16] {'col'}, use_global_device_ids=true, to_apply=%region_3.3 | all-reduce | flops 8192 | bytes 32768 | tf_op jit(solution)/shard_map/while/body/eval_jaxpr/psum | solution.py:11
  (94 shorter events, 490.0 us)
Async XLA Ops:
  0.0 25.0 %copy-start = (bf16[64,1,128,128]{3,2,1,0:T(8,128)(2,1)S(1)}, bf16[64,1,128,128]{3,2,1,0:T(8,128)(2,1)}, u32[]{:S(2)}) copy-start(bf16[64,1,128,128]{3,2,1,0:T(8,128)(2,1)} %param.11) | copy-start | bytes 6291460
  0.0 25.0 %copy-start.4 = (s32[64]{0:T(128)S(1)}, s32[64]{0:T(128)}, u32[]{:S(2)}) copy-start(s32[64]{0:T(128)} %param.13) | copy-start | bytes 772
  25.0 50.5 %copy-start.3 = (f32[1,64,128]{2,1,0:T(8,128)S(1)}, f32[1,64,128]{2,1,0:T(8,128)}, u32[]{:S(2)}) copy-start(f32[1,64,128]{2,1,0:T(8,128)} %param.8) | copy-start | bytes 98308
  25.0 50.6 %copy-start.1 = (f32[1,128,128]{2,1,0:T(8,128)S(1)}, f32[1,128,128]{2,1,0:T(8,128)}, u32[]{:S(2)}) copy-start(f32[1,128,128]{2,1,0:T(8,128)} %param.9) | copy-start | bytes 196612
  25.0 50.6 %copy-start.2 = (bf16[1,1,128,128]{3,2,1,0:T(8,128)(2,1)S(1)}, bf16[1,1,128,128]{3,2,1,0:T(8,128)(2,1)}, u32[]{:S(2)}) copy-start(bf16[1,1,128,128]{3,2,1,0:T(8,128)(2,1)} %param.10) | copy-start | bytes 98308
where the time goes:
time: 1930 us
  blocking collectives  1920 us (99%)
    psum x16, blocking collectives, spread(): return lax.psum(jnp.where(mine, array, jnp.zeros_like(array)), axis)  1120 us
    psum x16, blocking collectives, step_reduced(): lax.psum(partial_value.astype(jnp.bfloat16), 'row').astype(jnp.float32)  732 us
    psum x1, blocking collectives, body(): off_sum = lax.psum(off_part, 'row')  48.6 us

commit v1 on v0

--- a/solution.py
+++ b/solution.py
@@ -1,9 +1,25 @@
+import functools
 import jax
 import jax.numpy as jnp
 from jax import lax
 from jax.sharding import PartitionSpec as P
 
 NB = 16
+
+
+def desk_finish(v0, axis_key):
+    carry_in = v0
+    amount_of = lax.axis_size(axis_key)
+    for ii in [
+        [(pp, pp ^ dev_j) for pp in range(amount_of)]
+        for dev_j in (1, 2, 4, 8, 16)
+        if dev_j < amount_of
+    ]:
+        carry_in = carry_in + lax.ppermute(carry_in, axis_key, perm=ii)
+    return carry_in
+
+
+_guide_sources_all = functools.partial(desk_finish, axis_key="row")
 
 
 def spread(array, axis, root):
@@ -29,7 +45,7 @@
     known_row = lax.all_gather(known, "col", axis=0, tiled=True)
     picked = jnp.take(known_row, row_index, axis=0)
     off_part = jnp.einsum("pqi,pbia->bqa", picked, offdiag, preferred_element_type=jnp.float32)
-    off_sum = lax.psum(off_part, "row")
+    off_sum = _guide_sources_all(off_part)
     update = rhs - off_sum
     col_global = jnp.arange(col_slots) * cols_count + col_id
     accum = jnp.zeros(update.shape, jnp.float32)

time: 1930 us -> 1900 us (0.984)
  blocking collectives: 1920 us -> 1870 us
    psum x1 -> x0, blocking collectives: 48.6 us -> none  [body(): off_sum = lax.psum(off_part, 'row')]
  transfers between devices with their start and end apart: 0 -> 4, of which waited for: 0 -> 4; matrix products, arithmetic and copies ran while one was open for 0% -> 0% of each run, Pallas kernels for 0% -> 0%
where the time goes in v1:
time: 1900 us
  blocking collectives  1870 us (98%)
    psum x16, blocking collectives, spread(): return lax.psum(jnp.where(mine, array, jnp.zeros_like(array)), axis)  1120 us
    psum x16, blocking collectives, step_reduced(): lax.psum(partial_value.astype(jnp.bfloat16), 'row').astype(jnp.float32)  733 us
  transfers between devices with their start and end apart: 4, of which 4 were waited for; matrix products, arithmetic and copies ran while one was open for 0% of the time, Pallas kernels for 0%

profile of v1, /device:TPU:0, one launch (start us, length us, event | category | flops | bytes accessed | tf_op | source)
XLA Modules:
  0.0 1901.5 jit_solution(4550065972621105938)
XLA Ops:
  46.7 1854.1 %while.19 = (s32[]{:T(128)}, f32[1,64,128]{2,1,0:T(8,128)S(1)}, bf16[16,64,128]{2,1,0:T(8,128)(2,1)S(1)}, s32[1]{0:T(128)}, s32[]{:T(128)}, /*index=5*/f32[1,64,...) while((s32[]{:T(128)}, f32[1,64,128]{2,1,0:T(8,128)S(1)}, ...), condition=%wide.region_3.4_spmd.clone, body=%wide.region_0.3_spmd.clone.sunk | while | flops 14762007 | bytes 393562 | solution.py:68
  46.8 47.4 %psum.32 = bf16[64,128]{1,0:T(8,128)(2,1)S(1)} all-reduce(bf16[64,128]{1,0:T(8,128)(2,1)S(1)} %fusion.26), channel_id=1, replica_groups=mesh['row'=16,'col'=16] {'row'}, use_global_device_ids=true, to_apply=%region_1.1 | all-reduce | flops 8192 | bytes 32768 | tf_op jit(solution)/shard_map/while/body/eval_jaxpr/psum | solution.py:59
  94.3 72.1 %psum.33 = bf16[64,128]{1,0:T(8,128)(2,1)S(1)} all-reduce(bf16[64,128]{1,0:T(8,128)(2,1)S(1)} %fusion.27), channel_id=1, replica_groups=mesh['row'=16,'col'=16] {'col'}, use_global_device_ids=true, to_apply=%region_2.2 | all-reduce | flops 8192 | bytes 32768 | tf_op jit(solution)/shard_map/while/body/eval_jaxpr/psum | solution.py:27
  166.6 45.7 %psum.32 = bf16[64,128]{1,0:T(8,128)(2,1)S(1)} all-reduce(bf16[64,128]{1,0:T(8,128)(2,1)S(1)} %fusion.26), channel_id=1, replica_groups=mesh['row'=16,'col'=16] {'row'}, use_global_device_ids=true, to_apply=%region_1.1 | all-reduce | flops 8192 | bytes 32768 | tf_op jit(solution)/shard_map/while/body/eval_jaxpr/psum | solution.py:59
  212.5 69.6 %psum.33 = bf16[64,128]{1,0:T(8,128)(2,1)S(1)} all-reduce(bf16[64,128]{1,0:T(8,128)(2,1)S(1)} %fusion.27), channel_id=1, replica_groups=mesh['row'=16,'col'=16] {'col'}, use_global_device_ids=true, to_apply=%region_2.2 | all-reduce | flops 8192 | bytes 32768 | tf_op jit(solution)/shard_map/while/body/eval_jaxpr/psum | solution.py:27
  328.1 69.6 %psum.33 = bf16[64,128]{1,0:T(8,128)(2,1)S(1)} all-reduce(bf16[64,128]{1,0:T(8,128)(2,1)S(1)} %fusion.27), channel_id=1, replica_groups=mesh['row'=16,'col'=16] {'col'}, use_global_device_ids=true, to_apply=%region_2.2 | all-reduce | flops 8192 | bytes 32768 | tf_op jit(solution)/shard_map/while/body/eval_jaxpr/psum | solution.py:27
  443.7 69.6 %psum.33 = bf16[64,128]{1,0:T(8,128)(2,1)S(1)} all-reduce(bf16[64,128]{1,0:T(8,128)(2,1)S(1)} %fusion.27), channel_id=1, replica_groups=mesh['row'=16,'col'=16] {'col'}, use_global_device_ids=true, to_apply=%region_2.2 | all-reduce | flops 8192 | bytes 32768 | tf_op jit(solution)/shard_map/while/body/eval_jaxpr/psum | solution.py:27
  513.4 45.7 %psum.32 = bf16[64,128]{1,0:T(8,128)(2,1)S(1)} all-reduce(bf16[64,128]{1,0:T(8,128)(2,1)S(1)} %fusion.26), channel_id=1, replica_groups=mesh['row'=16,'col'=16] {'row'}, use_global_device_ids=true, to_apply=%region_1.1 | all-reduce | flops 8192 | bytes 32768 | tf_op jit(solution)/shard_map/while/body/eval_jaxpr/psum | solution.py:59
  559.3 69.6 %psum.33 = bf16[64,128]{1,0:T(8,128)(2,1)S(1)} all-reduce(bf16[64,128]{1,0:T(8,128)(2,1)S(1)} %fusion.27), channel_id=1, replica_groups=mesh['row'=16,'col'=16] {'col'}, use_global_device_ids=true, to_apply=%region_2.2 | all-reduce | flops 8192 | bytes 32768 | tf_op jit(solution)/shard_map/while/body/eval_jaxpr/psum | solution.py:27
  629.1 45.7 %psum.32 = bf16[64,128]{1,0:T(8,128)(2,1)S(1)} all-reduce(bf16[64,128]{1,0:T(8,128)(2,1)S(1)} %fusion.26), channel_id=1, replica_groups=mesh['row'=16,'col'=16] {'row'}, use_global_device_ids=true, to_apply=%region_1.1 | all-reduce | flops 8192 | bytes 32768 | tf_op jit(solution)/shard_map/while/body/eval_jaxpr/psum | solution.py:59
  675.0 69.6 %psum.33 = bf16[64,128]{1,0:T(8,128)(2,1)S(1)} all-reduce(bf16[64,128]{1,0:T(8,128)(2,1)S(1)} %fusion.27), channel_id=1, replica_groups=mesh['row'=16,'col'=16] {'col'}, use_global_device_ids=true, to_apply=%region_2.2 | all-reduce | flops 8192 | bytes 32768 | tf_op jit(solution)/shard_map/while/body/eval_jaxpr/psum | solution.py:27
  790.6 69.6 %psum.33 = bf16[64,128]{1,0:T(8,128)(2,1)S(1)} all-reduce(bf16[64,128]{1,0:T(8,128)(2,1)S(1)} %fusion.27), channel_id=1, replica_groups=mesh['row'=16,'col'=16] {'col'}, use_global_device_ids=true, to_apply=%region_2.2 | all-reduce | flops 8192 | bytes 32768 | tf_op jit(solution)/shard_map/while/body/eval_jaxpr/psum | solution.py:27
  860.3 45.7 %psum.32 = bf16[64,128]{1,0:T(8,128)(2,1)S(1)} all-reduce(bf16[64,128]{1,0:T(8,128)(2,1)S(1)} %fusion.26), channel_id=1, replica_groups=mesh['row'=16,'col'=16] {'row'}, use_global_device_ids=true, to_apply=%region_1.1 | all-reduce | flops 8192 | bytes 32768 | tf_op jit(solution)/shard_map/while/body/eval_jaxpr/psum | solution.py:59
  906.2 69.6 %psum.33 = bf16[64,128]{1,0:T(8,128)(2,1)S(1)} all-reduce(bf16[64,128]{1,0:T(8,128)(2,1)S(1)} %fusion.27), channel_id=1, replica_groups=mesh['row'=16,'col'=16] {'col'}, use_global_device_ids=true, to_apply=%region_2.2 | all-reduce | flops 8192 | bytes 32768 | tf_op jit(solution)/shard_map/while/body/eval_jaxpr/psum | solution.py:27
  975.9 45.7 %psum.32 = bf16[64,128]{1,0:T(8,128)(2,1)S(1)} all-reduce(bf16[64,128]{1,0:T(8,128)(2,1)S(1)} %fusion.26), channel_id=1, replica_groups=mesh['row'=16,'col'=16] {'row'}, use_global_device_ids=true, to_apply=%region_1.1 | all-reduce | flops 8192 | bytes 32768 | tf_op jit(solution)/shard_map/while/body/eval_jaxpr/psum | solution.py:59
  1021.8 69.6 %psum.33 = bf16[64,128]{1,0:T(8,128)(2,1)S(1)} all-reduce(bf16[64,128]{1,0:T(8,128)(2,1)S(1)} %fusion.27), channel_id=1, replica_groups=mesh['row'=16,'col'=16] {'col'}, use_global_device_ids=true, to_apply=%region_2.2 | all-reduce | flops 8192 | bytes 32768 | tf_op jit(solution)/shard_map/while/body/eval_jaxpr/psum | solution.py:27
  1137.4 69.6 %psum.33 = bf16[64,128]{1,0:T(8,128)(2,1)S(1)} all-reduce(bf16[64,128]{1,0:T(8,128)(2,1)S(1)} %fusion.27), channel_id=1, replica_groups=mesh['row'=16,'col'=16] {'col'}, use_global_device_ids=true, to_apply=%region_2.2 | all-reduce | flops 8192 | bytes 32768 | tf_op jit(solution)/shard_map/while/body/eval_jaxpr/psum | solution.py:27
  1207.1 45.7 %psum.32 = bf16[64,128]{1,0:T(8,128)(2,1)S(1)} all-reduce(bf16[64,128]{1,0:T(8,128)(2,1)S(1)} %fusion.26), channel_id=1, replica_groups=mesh['row'=16,'col'=16] {'row'}, use_global_device_ids=true, to_apply=%region_1.1 | all-reduce | flops 8192 | bytes 32768 | tf_op jit(solution)/shard_map/while/body/eval_jaxpr/psum | solution.py:59
  1253.1 69.6 %psum.33 = bf16[64,128]{1,0:T(8,128)(2,1)S(1)} all-reduce(bf16[64,128]{1,0:T(8,128)(2,1)S(1)} %fusion.27), channel_id=1, replica_groups=mesh['row'=16,'col'=16] {'col'}, use_global_device_ids=true, to_apply=%region_2.2 | all-reduce | flops 8192 | bytes 32768 | tf_op jit(solution)/shard_map/while/body/eval_jaxpr/psum | solution.py:27
  1368.7 69.6 %psum.33 = bf16[64,128]{1,0:T(8,128)(2,1)S(1)} all-reduce(bf16[64,128]{1,0:T(8,128)(2,1)S(1)} %fusion.27), channel_id=1, replica_groups=mesh['row'=16,'col'=16] {'col'}, use_global_device_ids=true, to_apply=%region_2.2 | all-reduce | flops 8192 | bytes 32768 | tf_op jit(solution)/shard_map/while/body/eval_jaxpr/psum | solution.py:27
  1484.3 69.6 %psum.33 = bf16[64,128]{1,0:T(8,128)(2,1)S(1)} all-reduce(bf16[64,128]{1,0:T(8,128)(2,1)S(1)} %fusion.27), channel_id=1, replica_groups=mesh['row'=16,'col'=16] {'col'}, use_global_device_ids=true, to_apply=%region_2.2 | all-reduce | flops 8192 | bytes 32768 | tf_op jit(solution)/shard_map/while/body/eval_jaxpr/psum | solution.py:27
  1599.9 69.6 %psum.33 = bf16[64,128]{1,0:T(8,128)(2,1)S(1)} all-reduce(bf16[64,128]{1,0:T(8,128)(2,1)S(1)} %fusion.27), channel_id=1, replica_groups=mesh['row'=16,'col'=16] {'col'}, use_global_device_ids=true, to_apply=%region_2.2 | all-reduce | flops 8192 | bytes 32768 | tf_op jit(solution)/shard_map/while/body/eval_jaxpr/psum | solution.py:27
  1715.5 69.6 %psum.33 = bf16[64,128]{1,0:T(8,128)(2,1)S(1)} all-reduce(bf16[64,128]{1,0:T(8,128)(2,1)S(1)} %fusion.27), channel_id=1, replica_groups=mesh['row'=16,'col'=16] {'col'}, use_global_device_ids=true, to_apply=%region_2.2 | all-reduce | flops 8192 | bytes 32768 | tf_op jit(solution)/shard_map/while/body/eval_jaxpr/psum | solution.py:27
  1831.2 69.6 %psum.33 = bf16[64,128]{1,0:T(8,128)(2,1)S(1)} all-reduce(bf16[64,128]{1,0:T(8,128)(2,1)S(1)} %fusion.27), channel_id=1, replica_groups=mesh['row'=16,'col'=16] {'col'}, use_global_device_ids=true, to_apply=%region_2.2 | all-reduce | flops 8192 | bytes 32768 | tf_op jit(solution)/shard_map/while/body/eval_jaxpr/psum | solution.py:27
  (102 shorter events, 464.0 us)
Async XLA Ops:
  0.0 25.6 %copy-start = (bf16[64,1,128,128]{3,2,1,0:T(8,128)(2,1)S(1)}, bf16[64,1,128,128]{3,2,1,0:T(8,128)(2,1)}, u32[]{:S(2)}) copy-start(bf16[64,1,128,128]{3,2,1,0:T(8,128)(2,1)} %param.11) | copy-start | bytes 6291460
  25.6 21.0 %copy-start.3 = (f32[1,64,128]{2,1,0:T(8,128)S(1)}, f32[1,64,128]{2,1,0:T(8,128)}, u32[]{:S(2)}) copy-start(f32[1,64,128]{2,1,0:T(8,128)} %param.8) | copy-start | bytes 98308
  25.7 21.0 %copy-start.1 = (f32[1,128,128]{2,1,0:T(8,128)S(1)}, f32[1,128,128]{2,1,0:T(8,128)}, u32[]{:S(2)}) copy-start(f32[1,128,128]{2,1,0:T(8,128)} %param.9) | copy-start | bytes 196612
  25.7 21.1 %copy-start.2 = (bf16[1,1,128,128]{3,2,1,0:T(8,128)(2,1)S(1)}, bf16[1,1,128,128]{3,2,1,0:T(8,128)(2,1)}, u32[]{:S(2)}) copy-start(bf16[1,1,128,128]{3,2,1,0:T(8,128)(2,1)} %param.10) | copy-start | bytes 98308
  27.5 1.3 collective-permute-start
  28.8 3.9 collective-permute-start.1
  32.7 5.2 collective-permute-start.2
  37.9 8.7 collective-permute-start.3
